TPU v7x, 32 devices: a whole 2x2x4 slice. The times are simulated.
32 devices in a mesh: row: 8 (over y, x, core), col: 4 (over z).
Axes of the slice: x: 2, y: 2, z: 4, core: 2. Of those that a mesh axis runs over, the one named last changes fastest.
Arguments:
- features: bfloat16 [512, 16384], P('col', 'row'), may hold values from -6 to 6
- weight: bfloat16 [512, 512], replicated, may hold values from -0.25 to 0.25
- tile_cols: int32 [8, 256], P('row'), may hold values from 0 to 127, as said below
- tile_rows: int32 [8, 256], P('row'), may hold values from 0 to 15
- tile_count: int32 [8], P('row'), may hold values from 1 to 256, as said below
- tile_values: bfloat16 [2048, 128, 128], P('row'), may hold values from 0 to 0.049804688
- out_grad: bfloat16 [512, 16384], P('col', 'row'), may hold values from -6 to 6
Outputs:
- output: bfloat16 [512, 16384], P('col', 'row')
- input_grad: bfloat16 [512, 16384], P('col', 'row')
- weight_grad: float32 [512, 512], P(None, 'col')
Inputs may be any that keep to these rules, and one draw needn't show every extreme that they name: `tile_cols`: the column tiles used by the slots t < tile_count[r] of row index r that lie in the range of one other row index s (tiles s * 16 to s * 16 + 15) are at most 4 distinct ones, and some pair r, s has exactly 4. Slots past tile_count[r] hold in-range entries that are not used. `tile_count`: some row index uses all 256 slots.
All inputs are finite; a program needn't handle non-finite values.
Results may differ from a plain program's by a relative error of at most 0.0061.
Values may be sent and summed in bfloat16 or wider, within the bound.
No kernel may reach another device: no remote copies, remote signals or barrier semaphores. Data moves between devices by JAX's collectives and lax.ppermute only.
A program may use at most 128 MiB of HBM per device.

v0:
```python
import jax
import jax.numpy as jnp
from jax import lax
from jax.sharding import PartitionSpec as P

TILE = 128


def shards(features, weight, tile_cols, tile_rows, tile_count, tile_values, out_grad):
    n_row = lax.axis_size("row")
    col_self = lax.axis_index("col")
    f_loc, nodes_loc = features.shape
    h_loc = out_grad.shape[0]
    row_tiles = nodes_loc // TILE
    max_tiles = tile_cols.shape[1]
    col_ids = tile_cols[0]
    row_ids = tile_rows[0]
    slot_ids = jnp.arange(max_tiles, dtype=jnp.int32)
    in_use = slot_ids < tile_count[0]
    all_feats = lax.all_gather(features, "col", axis=0, tiled=True)
    w_mine = lax.dynamic_slice_in_dim(weight, col_self * h_loc, h_loc, 1)
    projected = jnp.einsum("fh,fn->hn", w_mine, all_feats, preferred_element_type=jnp.float32)
    projected = projected.astype(jnp.bfloat16).reshape(h_loc, row_tiles, TILE)
    sources_table = lax.all_gather(projected, "row", axis=1, tiled=True)
    picked = jnp.take(sources_table, col_ids, axis=1)
    products = jnp.einsum("htm,tnm->thn", picked, tile_values, preferred_element_type=jnp.float32)
    placing = (
        (row_ids[:, None] == jnp.arange(row_tiles, dtype=jnp.int32)[None, :]) & in_use[:, None]
    ).astype(jnp.float32)
    preact = jnp.einsum("ti,thn->hin", placing, products, precision=lax.Precision.HIGHEST)
    logistic = jax.nn.sigmoid(preact)
    output = (preact * logistic).astype(jnp.bfloat16)
    slope_v = logistic * (1.0 + preact * (1.0 - logistic))
    z_grad = (out_grad.reshape(h_loc, row_tiles, TILE).astype(jnp.float32) * slope_v).astype(
        jnp.bfloat16
    )
    picked_z = jnp.take(z_grad, row_ids, axis=1)
    back_terms = jnp.einsum(
        "htn,tnm->thm", picked_z, tile_values, preferred_element_type=jnp.float32
    )
    back_terms = back_terms * in_use.astype(jnp.float32)[:, None, None]
    spread = jax.ops.segment_sum(back_terms, col_ids, num_segments=n_row * row_tiles)
    summed = lax.psum_scatter(spread, "row", scatter_dimension=0, tiled=True)
    p_grad = summed.astype(jnp.bfloat16)
    w_term = jnp.einsum(
        "fbn,bhn->fh",
        all_feats.reshape(all_feats.shape[0], row_tiles, TILE),
        p_grad,
        preferred_element_type=jnp.float32,
    )
    weight_grad = lax.psum(w_term, "row") * float(nodes_loc * n_row) ** (-0.5)
    w_rows = lax.dynamic_slice_in_dim(weight, col_self * f_loc, f_loc, 0)
    grad_sum = jnp.einsum(
        "fh,bhn->fbn",
        w_rows,
        lax.all_gather(p_grad, "col", axis=1, tiled=True),
        preferred_element_type=jnp.float32,
    )
    input_grad = grad_sum.astype(jnp.bfloat16).reshape(f_loc, nodes_loc)
    return (output.reshape(h_loc, nodes_loc), input_grad, weight_grad)


def solution(mesh):
    return jax.shard_map(
        shards,
        mesh=mesh,
        in_specs=(
            P("col", "row"),
            P(),
            P("row", None),
            P("row", None),
            P("row"),
            P("row", None, None),
            P("col", "row"),
        ),
        out_specs=(P("col", "row"), P("col", "row"), P(None, "col")),
        check_vma=False,
    )
```

profile of v0, /device:TPU:0, one launch (start us, length us, event | category | flops | bytes accessed | tf_op | source)
XLA Modules:
  0.0 408.7 jit_solution(3409858486664761841)
XLA Ops:
  7.2 2.1 copy.22
  9.4 0.0 all-gather.6.cloned.1.call-start
  9.4 49.7 %all-gather.4.cloned.1.call-done = bf16[512,2048]{0,1:T(8,128)(2,1)} async-done(((bf16[128,2048]{0,1:T(8,128)(2,1)}), bf16[512,2048]{0,1:T(8,128)(2,1)}) %all-gather.4.cloned.1.call-update) | async-done | bytes 2097168 | tf_op jit(solution)/shard_map/all_gather | solution.py:20
  59.1 2.4 fusion.14
  61.6 0.9 copy.45
  62.5 0.0 reduce-scatter.2.cloned.1.call-start
  63.2 1.1 convert_bitcast_fusion
  64.4 0.2 copy.35
  64.7 33.0 %all-gather.6.cloned.1.call-done = bf16[128,128,128]{2,0,1:T(8,128)(2,1)} async-done(((bf16[128,16,128]{2,0,1:T(8,128)(2,1)}), bf16[128,128,128]{2,0,1:T(8,128)(2,1)}) %all-gather.6.cloned.1.call-update) | async-done | bytes 4194320 | tf_op jit(solution)/shard_map/all_gather | solution.py:24
  97.6 10.8 %gather_fusion = bf16[256,128,128]{2,1,0:T(8,128)(2,1)} fusion(bf16[128,128,128]{2,0,1:T(8,128)(2,1)} %all-gather.6.cloned.1.call-done, s32[1024]{0:T(1024)S(1)} %pad_clamp_fusion.1), kind=kCustom, calls=%fused_computation | custom fusion | bytes 16778240 | tf_op jit(solution)/shard_map/jit(_take)/gather | solution.py:25
  108.4 12.8 %fusion.3 = f32[256,128,128]{2,1,0:T(8,128)} fusion(bf16[256,128,128]{2,1,0:T(8,128)(2,1)} %param.12, bf16[256,128,128]{2,1,0:T(8,128)(2,1)} %gather_fusion, pred[256]{0:T(512)(128)(4,1)S(1)} %compare_and_fusion.1), kind=kOutput, calls=%fused_computation.7 | convolution fusion | flops 1077936128 | bytes 33554688 | tf_op jit(solution)/shard_map/htm,tnm->thn/dot_general | solution.py:26
  121.2 14.1 %fusion.15 = (bf16[128,16,128]{2,1,0:T(8,128)(2,1)S(1)}, bf16[128,16,128]{2,1,0:T(8,128)(2,1)}) fusion(f32[16,8,16,128]{3,2,1,0:T(8,128)S(1)} %copy.35, s32[256]{0:T(256)S(1)} %bitcast.63, pred[256]{0:T(512)(128)(4,1)S(1)} %iota_compare_fusion.1, f32[256,128,128]{2,1,0:T(8,128)} %fusion.3), kind=kOutput, calls=%fused_computation.20 | convolution fusion | flops 808198144 | bytes 18875648 | tf_op jit(solution)/shard_map/ti,thn->hin/dot_general | solution.py:30
  135.3 0.1 copy.25
  135.4 8.6 %gather_fusion.1 = bf16[256,128,128]{2,1,0:T(8,128)(2,1)} fusion(bf16[128,16,128]{2,0,1:T(8,128)(2,1)S(1)} %copy.25, s32[1024]{0:T(1024)S(1)} %pad_clamp_fusion), kind=kCustom, calls=%fused_computation.1 | custom fusion | bytes 16778240 | tf_op jit(solution)/shard_map/jit(_take)/gather | solution.py:37
  144.1 14.0 %convolution_multiply_fusion = f32[256,128,128]{2,1,0:T(8,128)} fusion(bf16[256,128,128]{2,1,0:T(8,128)(2,1)} %param.12, bf16[256,128,128]{2,1,0:T(8,128)(2,1)} %gather_fusion.1, f32[256]{0:T(256)S(1)} %get-tuple-element.15, pred[256]{0:T(512)(128)(4,1)S(1)} %get-tuple-element.14), kind=kOutput, calls=%fused_computation.5 | convolution fusion | flops 1082130432 | bytes 33555712 | tf_op jit(solution)/shard_map/htn,tnm->thm/dot_general | solution.py:38
  158.1 4.3 %broadcast_in_dim.26 = f32[128,128,128]{2,1,0:T(8,128)} broadcast(f32[]{:T(128)} %constant.40.clone.1), dimensions={} | broadcast | bytes 8388612 | tf_op jit(solution)/shard_map/broadcast_in_dim | solution.py:42
  162.4 51.3 %scatter_fusion = f32[128,128,128]{2,1,0:T(8,128)} fusion(f32[128,128,128]{2,1,0:T(8,128)} %broadcast_in_dim.26, s32[256]{0:T(256)S(1)} %bitcast.65, f32[256,128,128]{2,1,0:T(8,128)} %convolution_multiply_fusion), kind=kCustom, calls=%fused_computation.2 | custom fusion | flops 4194304 | bytes 50332672 | tf_op jit(solution)/shard_map/scatter-add | solution.py:42
  213.6 9.0 %copy.26 = f32[128,128,128]{1,2,0:T(8,128)} copy(f32[128,128,128]{2,1,0:T(8,128)} %scatter_fusion) | data formatting | bytes 16777216 | tf_op jit(solution)/shard_map/scatter-add | solution.py:42
  222.7 0.0 all-reduce.2.cloned.1.call-start
  222.7 71.6 %reduce-scatter.2.cloned.1.call-done = f32[16,128,128]{1,2,0:T(8,128)} async-done(((f32[128,128,128]{1,2,0:T(8,128)}), f32[16,128,128]{1,2,0:T(8,128)}) %reduce-scatter.2.cloned.1.call-update) | async-done | bytes 1048592 | tf_op jit(solution)/shard_map/reduce_scatter | solution.py:43
  294.3 1.3 convert_element_type.35
  295.6 1.2 convolution_bitcast_fusion
  296.8 0.0 all-gather.8.cloned.1.call-start
  296.9 0.5 all-gather.8.cloned.1.call-update
  297.4 2.0 copy.44
  299.4 52.3 %all-reduce.2.cloned.1.call-done = f32[512,128]{0,1:T(8,128)} async-done(((f32[512,128]{0,1:T(8,128)}), f32[512,128]{0,1:T(8,128)}) %all-reduce.2.cloned.1.call-update) | async-done | bytes 262160 | tf_op jit(solution)/shard_map/psum | solution.py:51
  351.7 1.0 broadcast_multiply_fusion
  352.6 0.8 copy.30
  353.5 45.3 %all-gather.8.cloned.1.call-done = bf16[16,512,128]{1,2,0:T(8,128)(2,1)} async-done(((bf16[16,128,128]{1,2,0:T(8,128)(2,1)}), bf16[16,512,128]{1,2,0:T(8,128)(2,1)}) %all-gather.8.cloned.1.call-update) | async-done | bytes 2097168 | tf_op jit(solution)/shard_map/all_gather | solution.py:56
  398.7 2.3 fusion.16
  401.0 0.1 convert_element_type.36
  401.1 1.0 copy.29
  (22 shorter events, 0.2 us)
Async XLA Ops:
  7.2 52.0 %copy-start = (bf16[512,512]{1,0:T(8,128)(2,1)S(1)}, bf16[512,512]{1,0:T(8,128)(2,1)}, u32[]{:S(2)}) copy-start(bf16[512,512]{1,0:T(8,128)(2,1)} %param.8) | copy-start | bytes 1572868
  7.2 57.4 %copy-start.3 = (s32[1,256]{1,0:T(1,128)S(1)}, s32[1,256]{1,0:T(1,128)}, u32[]{:S(2)}) copy-start(s32[1,256]{1,0:T(1,128)} %param.10) | copy-start | bytes 3076
  7.2 57.4 %copy-start.4 = (s32[1,256]{1,0:T(1,128)S(1)}, s32[1,256]{1,0:T(1,128)}, u32[]{:S(2)}) copy-start(s32[1,256]{1,0:T(1,128)} %param.9) | copy-start | bytes 3076
  7.2 51.9 %all-gather.4.cloned.1.call-start = ((), (), s32[]{:S(2)}) async-start(), calls=%async_computation.1 | async-start | bytes 2621440 | tf_op jit(solution)/shard_map/all_gather | solution.py:20
  9.4 88.3 %all-gather.6.cloned.1.call-start = ((), (), s32[]{:S(2)}) async-start(), calls=%async_computation.2 | async-start | bytes 4718592 | tf_op jit(solution)/shard_map/all_gather | solution.py:24
  62.5 231.8 %reduce-scatter.2.cloned.1.call-start = ((), (), s32[]{:S(2)}) async-start(), calls=%async_computation.3 | async-start | bytes 9437184 | tf_op jit(solution)/shard_map/reduce_scatter | solution.py:43
  222.6 73.0 %copy-start.1 = (bf16[512,2048]{0,1:T(8,128)(2,1)S(1)}, bf16[512,2048]{0,1:T(8,128)(2,1)}, u32[]{:S(2)}) copy-start(bf16[512,2048]{0,1:T(8,128)(2,1)} %all-gather.4.cloned.1.call-done) | copy-start | bytes 6291460
  222.7 129.0 %all-reduce.2.cloned.1.call-start = ((), (), s32[]{:S(2)}) async-start(), calls=%async_computation.5 | async-start | bytes 524288 | tf_op jit(solution)/shard_map/psum | solution.py:51
  295.6 1.3 copy-start.2
  296.8 101.9 %all-gather.8.cloned.1.call-start = ((), (), s32[]{:S(2)}) async-start(), calls=%async_computation.4 | async-start | bytes 2621440 | tf_op jit(solution)/shard_map/all_gather | solution.py:56
Sparse Core Ops, SparseCore 0:
  10.2 48.9 all-gather.3
  62.6 34.9 all-gather.5
  222.8 71.4 reduce-scatter.1
  298.1 53.5 all-reduce.1
  353.1 45.6 all-gather.7
where the time goes:
time: 410 us; the launch traced here: 409 us
  waiting for transfers between devices  252 us (61%)
  other arithmetic  54.8 us (13%)
  matrix products  46.8 us (11%)
  local copies, waits for them, and re-layouts  39.9 us (10%)
  between operations  14.6 us (4%)
    reduce_scatter x1, waiting for transfers between devices, shards(): summed = lax.psum_scatter(spread, 'row', scatter_dimension=0, tiled=True)  71.6 us
    psum x1, waiting for transfers between devices, shards(): weight_grad = lax.psum(w_term, 'row') * float(nodes_loc * n_row) ** (-0.5)  52.3 us
    scatter-add x1, other arithmetic, shards(): jax.ops.segment_sum(back_terms, col_ids, num_segments=n_row * row_tiles)  51.3 us
    all_gather x1, waiting for transfers between devices, shards(): all_feats = lax.all_gather(features, 'col', axis=0, tiled=True)  49.7 us
    all_gather x1, waiting for transfers between devices, shards(): lax.all_gather(p_grad, 'col', axis=1, tiled=True)  45.3 us
    all_gather x1, waiting for transfers between devices, shards(): sources_table = lax.all_gather(projected, 'row', axis=1, tiled=True)  33 us
    dot_general x1, matrix products, shards(): jnp.einsum('ti,thn->hin', placing, products, precision=lax.Precision.HIGH...  14.1 us
    dot_general x1, matrix products, shards(): jnp.einsum('htn,tnm->thm', picked_z, tile_values, preferred_element_type=...  14 us
  transfers between devices with their start and end apart: 5, of which 5 were waited for; matrix products, arithmetic and copies ran while one was open for 1% of the time, Pallas kernels for 0%

commit v1 on v0

--- a/solution.py
+++ b/solution.py
@@ -48,7 +48,9 @@
         p_grad,
         preferred_element_type=jnp.float32,
     )
-    weight_grad = lax.psum(w_term, "row") * float(nodes_loc * n_row) ** (-0.5)
+    weight_grad = jnp.sum(lax.all_gather(w_term, "row"), axis=0) * float(nodes_loc * n_row) ** (
+        -0.5
+    )
     w_rows = lax.dynamic_slice_in_dim(weight, col_self * f_loc, f_loc, 0)
     grad_sum = jnp.einsum(
         "fh,bhn->fbn",

time: 410 us -> 383 us (0.934)
  waiting for transfers between devices: 252 us -> 223 us
    psum x1 -> x0, waiting for transfers between devices: 52.3 us -> none  [shards(): weight_grad = lax.psum(w_term, 'row') * float(nodes_loc * n_row) ** (-0.5)]
    all_gather x0 -> x1, waiting for transfers between devices: none -> 25.2 us  [shards(): lax.all_gather(w_term, 'row')]
    unnamed x15 -> x14, local copies, waits for them, and re-layouts: 6.12 us -> 8.3 us
  transfers between devices with their start and end apart: 5 -> 5, of which waited for: 5 -> 5; matrix products, arithmetic and copies ran while one was open for 1% -> 2% of each run, Pallas kernels for 0% -> 0%
where the time goes in v1:
time: 383 us; the launch traced here: 382 us
  waiting for transfers between devices  223 us (58%)
  other arithmetic  55.3 us (14%)
  matrix products  47 us (12%)
  local copies, waits for them, and re-layouts  42 us (11%)
  between operations  14.6 us (4%)
    reduce_scatter x1, waiting for transfers between devices, shards(): summed = lax.psum_scatter(spread, 'row', scatter_dimension=0, tiled=True)  71.7 us
    scatter-add x1, other arithmetic, shards(): jax.ops.segment_sum(back_terms, col_ids, num_segments=n_row * row_tiles)  51.4 us
    all_gather x1, waiting for transfers between devices, shards(): all_feats = lax.all_gather(features, 'col', axis=0, tiled=True)  49.7 us
    all_gather x1, waiting for transfers between devices, shards(): lax.all_gather(p_grad, 'col', axis=1, tiled=True)  43.1 us
    all_gather x1, waiting for transfers between devices, shards(): sources_table = lax.all_gather(projected, 'row', axis=1, tiled=True)  33 us
    all_gather x1, waiting for transfers between devices, shards(): lax.all_gather(w_term, 'row')  25.2 us
    dot_general x1, matrix products, shards(): jnp.einsum('htn,tnm->thm', picked_z, tile_values, preferred_element_type=...  14 us
    dot_general x1, matrix products, shards(): jnp.einsum('ti,thn->hin', placing, products, precision=lax.Precision.HIGH...  13.3 us
  transfers between devices with their start and end apart: 5, of which 5 were waited for; matrix products, arithmetic and copies ran while one was open for 2% of the time, Pallas kernels for 0%

profile of v1, /device:TPU:0, one launch (start us, length us, event | category | flops | bytes accessed | tf_op | source)
XLA Modules:
  0.0 382.1 jit_solution(467316190072736975)
XLA Ops:
  7.2 2.1 copy.20
  9.4 0.0 all-gather.8.cloned.1.call-start
  9.4 49.7 %all-gather.6.cloned.1.call-done = bf16[512,2048]{0,1:T(8,128)(2,1)} async-done(((bf16[128,2048]{0,1:T(8,128)(2,1)}), bf16[512,2048]{0,1:T(8,128)(2,1)}) %all-gather.6.cloned.1.call-update) | async-done | bytes 2097168 | tf_op jit(solution)/shard_map/all_gather | solution.py:20
  59.1 2.4 fusion.14
  61.6 0.9 copy.44
  62.5 0.0 reduce-scatter.2.cloned.1.call-start
  63.2 1.1 convert_bitcast_fusion
  64.4 0.2 copy.33
  64.7 33.0 %all-gather.8.cloned.1.call-done = bf16[128,128,128]{2,0,1:T(8,128)(2,1)} async-done(((bf16[128,16,128]{2,0,1:T(8,128)(2,1)}), bf16[128,128,128]{2,0,1:T(8,128)(2,1)}) %all-gather.8.cloned.1.call-update) | async-done | bytes 4194320 | tf_op jit(solution)/shard_map/all_gather | solution.py:24
  97.6 10.8 %gather_fusion = bf16[256,128,128]{2,1,0:T(8,128)(2,1)} fusion(bf16[128,128,128]{2,0,1:T(8,128)(2,1)} %all-gather.8.cloned.1.call-done, s32[1024]{0:T(1024)S(1)} %pad_clamp_fusion.1), kind=kCustom, calls=%fused_computation | custom fusion | bytes 16778240 | tf_op jit(solution)/shard_map/jit(_take)/gather | solution.py:25
  108.4 12.8 %fusion.3 = f32[256,128,128]{2,1,0:T(8,128)} fusion(bf16[256,128,128]{2,1,0:T(8,128)(2,1)} %param.12, bf16[256,128,128]{2,1,0:T(8,128)(2,1)} %gather_fusion, pred[256]{0:T(512)(128)(4,1)S(1)} %compare_and_fusion.1), kind=kOutput, calls=%fused_computation.7 | convolution fusion | flops 1077936128 | bytes 33554688 | tf_op jit(solution)/shard_map/htm,tnm->thn/dot_general | solution.py:26
  121.2 13.3 %fusion.15 = (bf16[128,16,128]{2,1,0:T(8,128)(2,1)S(1)}, bf16[128,16,128]{2,1,0:T(8,128)(2,1)S(1)}) fusion(f32[16,8,16,128]{3,2,1,0:T(8,128)S(1)} %copy.33, s32[256]{0:T(256)S(1)} %bitcast.69, pred[256]{0:T(512)(128)(4,1)S(1)} %iota_compare_fusion.1, f32[256,128,128]{2,1,0:T(8,128)} %fusion.3), kind=kOutput, calls=%fused_computation.21 | convolution fusion | flops 808198144 | bytes 18875648 | tf_op jit(solution)/shard_map/ti,thn->hin/dot_general | solution.py:30
  134.5 0.1 copy.23
  134.6 8.6 %gather_fusion.1 = bf16[256,128,128]{2,1,0:T(8,128)(2,1)} fusion(bf16[128,16,128]{2,0,1:T(8,128)(2,1)S(1)} %copy.23, s32[1024]{0:T(1024)S(1)} %pad_clamp_fusion), kind=kCustom, calls=%fused_computation.1 | custom fusion | bytes 16778240 | tf_op jit(solution)/shard_map/jit(_take)/gather | solution.py:37
  143.2 14.0 %convolution_multiply_fusion = f32[256,128,128]{2,1,0:T(8,128)} fusion(bf16[256,128,128]{2,1,0:T(8,128)(2,1)} %param.12, bf16[256,128,128]{2,1,0:T(8,128)(2,1)} %gather_fusion.1, f32[256]{0:T(256)S(1)} %get-tuple-element.15, pred[256]{0:T(512)(128)(4,1)S(1)} %get-tuple-element.14), kind=kOutput, calls=%fused_computation.5 | convolution fusion | flops 1082130432 | bytes 33555712 | tf_op jit(solution)/shard_map/htn,tnm->thm/dot_general | solution.py:38
  157.3 4.3 %broadcast_in_dim.26 = f32[128,128,128]{2,1,0:T(8,128)} broadcast(f32[]{:T(128)} %constant.26.clone.1), dimensions={} | broadcast | bytes 8388612 | tf_op jit(solution)/shard_map/broadcast_in_dim | solution.py:42
  161.5 51.4 %scatter_fusion = f32[128,128,128]{2,1,0:T(8,128)} fusion(f32[128,128,128]{2,1,0:T(8,128)} %broadcast_in_dim.26, s32[256]{0:T(256)S(1)} %bitcast.71, f32[256,128,128]{2,1,0:T(8,128)} %convolution_multiply_fusion), kind=kCustom, calls=%fused_computation.2 | custom fusion | flops 4194304 | bytes 50332672 | tf_op jit(solution)/shard_map/scatter-add | solution.py:42
  212.9 9.0 %copy.24 = f32[128,128,128]{1,2,0:T(8,128)} copy(f32[128,128,128]{2,1,0:T(8,128)} %scatter_fusion) | data formatting | bytes 16777216 | tf_op jit(solution)/shard_map/scatter-add | solution.py:42
  222.0 0.0 all-gather.10.cloned.1.call-start
  222.0 71.7 %reduce-scatter.2.cloned.1.call-done = f32[16,128,128]{1,2,0:T(8,128)} async-done(((f32[128,128,128]{1,2,0:T(8,128)}), f32[16,128,128]{1,2,0:T(8,128)}) %reduce-scatter.2.cloned.1.call-update) | async-done | bytes 1048592 | tf_op jit(solution)/shard_map/reduce_scatter | solution.py:43
  293.8 2.1 convert_element_type.35
  295.9 0.0 all-gather.12.cloned.1.call-start
  296.0 2.2 convolution_bitcast_fusion
  298.2 0.9 copy.43
  299.1 43.1 %all-gather.10.cloned.1.call-done = bf16[16,512,128]{1,2,0:T(8,128)(2,1)} async-done(((bf16[16,128,128]{1,2,0:T(8,128)(2,1)}), bf16[16,512,128]{1,2,0:T(8,128)(2,1)}) %all-gather.10.cloned.1.call-update) | async-done | bytes 2097168 | tf_op jit(solution)/shard_map/all_gather | solution.py:58
  342.3 2.3 fusion.16
  344.6 0.1 convert_element_type.36
  344.7 1.0 copy.27
  345.7 25.2 %all-gather.12.cloned.1.call-done = f32[4096,128]{0,1:T(8,128)} async-done(((f32[512,128]{0,1:T(8,128)}), f32[4096,128]{0,1:T(8,128)}) %all-gather.12.cloned.1.call-update) | async-done | bytes 2097168 | tf_op jit(solution)/shard_map/all_gather | solution.py:51
  370.9 3.2 copy.34
  374.2 0.5 bitcast_reduce_fusion
  374.7 0.8 copy.28
  (22 shorter events, 0.2 us)
Async XLA Ops:
  7.2 52.0 %copy-start = (bf16[512,512]{1,0:T(8,128)(2,1)S(1)}, bf16[512,512]{1,0:T(8,128)(2,1)}, u32[]{:S(2)}) copy-start(bf16[512,512]{1,0:T(8,128)(2,1)} %param.8) | copy-start | bytes 1572868
  7.2 57.4 %copy-start.2 = (s32[1,256]{1,0:T(1,128)S(1)}, s32[1,256]{1,0:T(1,128)}, u32[]{:S(2)}) copy-start(s32[1,256]{1,0:T(1,128)} %param.10) | copy-start | bytes 3076
  7.2 57.4 %copy-start.3 = (s32[1,256]{1,0:T(1,128)S(1)}, s32[1,256]{1,0:T(1,128)}, u32[]{:S(2)}) copy-start(s32[1,256]{1,0:T(1,128)} %param.9) | copy-start | bytes 3076
  7.2 51.9 %all-gather.6.cloned.1.call-start = ((), (), s32[]{:S(2)}) async-start(), calls=%async_computation.1 | async-start | bytes 2621440 | tf_op jit(solution)/shard_map/all_gather | solution.py:20
  9.4 88.3 %all-gather.8.cloned.1.call-start = ((), (), s32[]{:S(2)}) async-start(), calls=%async_computation.2 | async-start | bytes 4718592 | tf_op jit(solution)/shard_map/all_gather | solution.py:24
  62.5 231.3 %reduce-scatter.2.cloned.1.call-start = ((), (), s32[]{:S(2)}) async-start(), calls=%async_computation.3 | async-start | bytes 9437184 | tf_op jit(solution)/shard_map/reduce_scatter | solution.py:43
  221.9 74.0 %copy-start.1 = (bf16[512,2048]{0,1:T(8,128)(2,1)S(1)}, bf16[512,2048]{0,1:T(8,128)(2,1)}, u32[]{:S(2)}) copy-start(bf16[512,2048]{0,1:T(8,128)(2,1)} %all-gather.6.cloned.1.call-done) | copy-start | bytes 6291460
  222.0 120.3 %all-gather.10.cloned.1.call-start = ((), (), s32[]{:S(2)}) async-start(), calls=%async_computation.4 | async-start | bytes 2621440 | tf_op jit(solution)/shard_map/all_gather | solution.py:58
  295.9 75.0 %all-gather.12.cloned.1.call-start = ((), (), s32[]{:S(2)}) async-start(), calls=%async_computation.5 | async-start | bytes 2359296 | tf_op jit(solution)/shard_map/all_gather | solution.py:51
Sparse Core Ops, SparseCore 0:
  10.2 48.9 all-gather.5
  62.6 34.9 all-gather.7
  222.1 71.6 reduce-scatter.1
  296.0 46.1 all-gather.9
  344.8 26.1 all-gather.11
